TPU v7x, 128 devices: a whole 4x4x4 slice. The times are simulated.
128 devices in a mesh: group: 16 (over x, z_hi, core), inner: 8 (over z_lo, y).
Axes of the slice: x: 4, y: 4, z: 4 (z_hi: 2, z_lo: 2; z = z_hi * 2 + z_lo), core: 2. Of those that a mesh axis runs over, the one named last changes fastest.
Arguments:
- tokens: bfloat16 [16, 512, 2304], P('group', 'inner'), may hold values from -6 to 6
- lengths: int32 [16], P('group'), may hold values from 1 to 512, 5120 in all
- tenant_cut: int32 [16], P('group'), may hold values from 64 to 255
- expert_ids: int32 [16, 512, 2], P('group', 'inner'), may hold values from 0 to 7, all different within a row; in each aligned block of 64 rows (0 to 63, 64 to 127, ..., all dimensions but the last counted through in order) at most 20 rows name the same one
- trainer_qkv: float32 [2304, 3, 2048], P(('group', 'inner')), may hold values from -0.26 to 0.26
- trainer_gate_up: float32 [8, 2304, 2, 5760], P(None, ('group', 'inner')), may hold values from -0.125 to 0.125
- out_weight: bfloat16 [2048, 2304], P('inner'), may hold values from -0.75 to 0.75
- down_weight: bfloat16 [8, 5760, 2304], P('inner', 'group'), may hold values from -0.078125 to 0.078125
- attn_gain: float32 [2304], replicated, may hold values from 0.1 to 1.9
- moe_gain: float32 [2304], replicated, may hold values from 0.1 to 1.9
- router: bfloat16 [2304, 8], replicated, may hold values from -0.375 to 0.375
Outputs:
- server_qkv: bfloat16 [2304, 3, 2048], P(None, None, 'inner')
- server_gate_up: bfloat16 [8, 2304, 2, 5760], P('inner', None, None, 'group')
- layer_out: bfloat16 [16, 512, 2304], P('group', 'inner')
Inputs may be any that keep to these rules, and one draw needn't show every extreme that they name: `expert_ids`: in each aligned block of 64 token slots (the slots of one device) no expert is named more than 20 times, a bound that some block reaches. The two experts of a slot differ. `lengths`: some prompt uses all 512 slots.
All inputs are finite; a program needn't handle non-finite values. No bound on the sum of `lengths` on one device may be relied on, other than what follows from the above.
Results may differ from a plain program's by a relative error of at most 0.015.
Values may be sent and summed in bfloat16 or wider, within the bound.
A program may use at most 128 MiB of HBM per device.

v0:
```python
import math
import jax
import jax.numpy as jnp
from jax import lax
from jax.sharding import PartitionSpec as P

D = 2304
HEAD_DIM = 64
TOPK = 2
NORM_EPS = 1e-05
MASKED = -1e30


def rms_scaled(values, gain_row):
    mean_square = jnp.mean(values * values, axis=-1, keepdims=True)
    return values * lax.rsqrt(mean_square + NORM_EPS) * gain_row


def token_layout(length, cut_point, total):
    places = jnp.arange(total, dtype=jnp.int32)
    beyond = places >= length
    second = places >= cut_point
    starts = jnp.where(beyond, length, jnp.where(second, cut_point, 0))
    tenants = jnp.where(beyond, 2, jnp.where(second, 1, 0))
    return (places - starts, tenants, places)


def rotate_heads(values, positions):
    half_dim = values.shape[-1] // 2
    freqs = jnp.exp(-math.log(10000.0) * jnp.arange(half_dim, dtype=jnp.float32) / half_dim)
    angles = positions.astype(jnp.float32)[:, None] * freqs[None, :]
    cosine = jnp.cos(angles)[:, None, :]
    sine = jnp.sin(angles)[:, None, :]
    first_half = values[..., :half_dim]
    second_half = values[..., half_dim:]
    return jnp.concatenate(
        [first_half * cosine - second_half * sine, second_half * cosine + first_half * sine],
        axis=-1,
    )


def body(
    tokens,
    lengths,
    tenant_cut,
    expert_ids,
    trainer_qkv,
    trainer_gate_up,
    out_weight,
    down_weight,
    attn_gain,
    moe_gain,
    router,
):
    group_size = lax.axis_size("group")
    inner_size = lax.axis_size("inner")
    row_share = trainer_qkv.shape[0]
    head_block = trainer_qkv.shape[2] // inner_size
    cast_qkv = trainer_qkv.astype(jnp.bfloat16).reshape(row_share, 3, inner_size, head_block)
    head_parts = lax.all_to_all(cast_qkv, "inner", split_axis=2, concat_axis=0, tiled=True)
    head_parts = head_parts.reshape(inner_size * row_share, 3, head_block)
    server_qkv = lax.all_gather(head_parts, "group", axis=0, tiled=True)
    expert_count = trainer_gate_up.shape[0]
    local_experts = expert_count // inner_size
    hidden_share = trainer_gate_up.shape[3] // group_size
    cast_gate_up = trainer_gate_up.astype(jnp.bfloat16).reshape(
        inner_size, local_experts, row_share, 2, group_size, hidden_share
    )
    ordered = jnp.transpose(cast_gate_up, (4, 0, 1, 2, 3, 5))
    joined = ordered.reshape(group_size * inner_size, local_experts, 1, row_share, 2, hidden_share)
    moved = lax.all_to_all(joined, ("group", "inner"), split_axis=0, concat_axis=2, tiled=True)
    server_gate_up = moved.reshape(local_experts, D, 2, hidden_share)
    tok_rows = tokens.shape[1]
    own_inputs = tokens[0].astype(jnp.float32)
    normed = rms_scaled(own_inputs, attn_gain).astype(jnp.bfloat16)
    length = lengths[0]
    cut_point = tenant_cut[0]
    heads_here = head_block // HEAD_DIM
    flat_qkv = server_qkv.reshape(D, 3 * head_block)
    piece_rows = lax.all_gather(normed, "inner", axis=0, tiled=True)
    row_count = piece_rows.shape[0]
    raw = jnp.dot(piece_rows, flat_qkv, preferred_element_type=jnp.float32).reshape(
        row_count, 3, heads_here, HEAD_DIM
    )
    positions, unused_tenants, unused_places = token_layout(length, cut_point, row_count)
    queries = rotate_heads(raw[:, 0], positions).astype(jnp.bfloat16)
    keys_rot = rotate_heads(raw[:, 1], positions).astype(jnp.bfloat16)
    values_v = raw[:, 2].astype(jnp.bfloat16)
    packed = jnp.stack([queries, keys_rot, values_v], axis=1).reshape(row_count, 3, head_block)
    seq_len = packed.shape[0]
    packed = packed.reshape(seq_len, 3, heads_here, HEAD_DIM)
    queries = packed[:, 0]
    keys_rot = packed[:, 1]
    values_v = packed[:, 2]
    unused_positions, tenants, places = token_layout(length, cut_point, seq_len)
    block_rows = min(seq_len, 512)
    scores = jnp.einsum(
        "qhd,khd->hqk", queries, keys_rot, preferred_element_type=jnp.float32
    ) / math.sqrt(HEAD_DIM)
    allowed = (tenants[0:block_rows, None] == tenants[None, :]) & (
        places[None, :] <= places[0:block_rows, None]
    )
    scores = jnp.where(allowed[None], scores, MASKED)
    weights = jax.nn.softmax(scores, axis=-1).astype(jnp.bfloat16)
    mixed = jnp.einsum("hqk,khd->qhd", weights, values_v, preferred_element_type=jnp.float32)
    block_outputs = mixed.astype(jnp.bfloat16).reshape(block_rows, head_block)
    projected = lax.psum_scatter(
        jnp.dot(block_outputs, out_weight, preferred_element_type=jnp.float32),
        "inner",
        scatter_dimension=0,
        tiled=True,
    )
    residual = own_inputs + projected
    normed_moe = rms_scaled(residual, moe_gain).astype(jnp.bfloat16)
    logits = jnp.dot(normed_moe, router, preferred_element_type=jnp.float32)
    route_ids = expert_ids[0]
    expert_range = jnp.arange(expert_count, dtype=jnp.int32)
    onehot = route_ids[:, :, None] == expert_range[None, None, :]
    chosen = jnp.sum(jnp.where(onehot, logits[:, None, :], 0.0), axis=-1)
    first_weight = jax.nn.sigmoid(chosen[:, 0] - chosen[:, 1])
    capacity = tok_rows * 5 // 16
    flat_hot = onehot.reshape(tok_rows * TOPK, expert_count).astype(jnp.int32)
    ranks = jnp.cumsum(flat_hot, axis=0) - flat_hot
    slot_ids = jnp.sum((expert_range[None, :] * capacity + ranks) * flat_hot, axis=1)
    slot_range = jnp.arange(expert_count * capacity, dtype=jnp.int32)
    dispatch = (slot_ids[None, :] == slot_range[:, None]).astype(jnp.bfloat16)
    repeated = jnp.broadcast_to(normed_moe[:, None, :], (tok_rows, TOPK, D)).reshape(
        tok_rows * TOPK, D
    )
    send_rows = jnp.dot(dispatch, repeated, preferred_element_type=jnp.float32).astype(jnp.bfloat16)
    send_rows = send_rows.reshape(inner_size, local_experts, capacity, D)
    owned = lax.all_to_all(send_rows, "inner", split_axis=0, concat_axis=0, tiled=True)
    arrived = lax.all_gather(owned, "group", axis=0, tiled=True)
    item_count = arrived.shape[0]
    rows_in = arrived[:, 0].reshape(item_count * capacity, D)
    both = jnp.dot(
        rows_in, server_gate_up[0].reshape(D, 2 * hidden_share), preferred_element_type=jnp.float32
    )
    both = both.reshape(item_count * capacity, 2, hidden_share)
    hidden = (jax.nn.silu(both[:, 0]) * both[:, 1]).astype(jnp.bfloat16)
    down_part = jnp.dot(hidden, down_weight[0], preferred_element_type=jnp.float32)
    results = [down_part.reshape(item_count, capacity, D)]
    terms = jnp.stack(results, axis=1).astype(jnp.bfloat16)
    summed = lax.psum_scatter(terms, "group", scatter_dimension=0, tiled=True).astype(jnp.float32)
    expert_out = lax.all_to_all(
        summed.astype(jnp.bfloat16), "inner", split_axis=0, concat_axis=0, tiled=True
    )
    flat_out = expert_out.reshape(expert_count * capacity, D)
    route_slots = slot_ids.reshape(tok_rows, TOPK)
    pick_first = (route_slots[:, 0:1] == slot_range[None, :]).astype(jnp.bfloat16)
    pick_second = (route_slots[:, 1:2] == slot_range[None, :]).astype(jnp.bfloat16)
    first_out = jnp.dot(pick_first, flat_out, preferred_element_type=jnp.float32)
    second_out = jnp.dot(pick_second, flat_out, preferred_element_type=jnp.float32)
    moe = first_weight[:, None] * first_out + (1.0 - first_weight)[:, None] * second_out
    combined = residual + moe
    own_places = lax.axis_index("inner") * tok_rows + jnp.arange(tok_rows, dtype=jnp.int32)
    layer_out = jnp.where((own_places < length)[:, None], combined, 0.0).astype(jnp.bfloat16)
    return (server_qkv, server_gate_up, layer_out[None])


def solution(mesh):
    placed = (
        P("group", "inner", None),
        P("group"),
        P("group"),
        P("group", "inner", None),
        P(("group", "inner"), None, None),
        P(None, ("group", "inner"), None, None),
        P("inner", None),
        P("inner", "group", None),
        P(),
        P(),
        P(),
    )
    return jax.shard_map(
        body,
        mesh=mesh,
        in_specs=placed,
        out_specs=(
            P(None, None, "inner"),
            P("inner", None, None, "group"),
            P("group", "inner", None),
        ),
        check_vma=False,
    )
```

profile of v0, /device:TPU:1, one launch (start us, length us, event | category | flops | bytes accessed | tf_op | source)
XLA Modules:
  0.0 555.8 jit_solution(7805670884036663510)
XLA Ops:
  7.2 1.3 convert_element_type.68
  8.9 12.7 %all_to_all.34 = bf16[18,3,8,256]{3,0,1,2:T(8,128)(2,1)S(1)} all-to-all(bf16[18,3,8,256]{3,0,1,2:T(8,128)(2,1)S(1)} %copy.52), channel_id=1, replica_groups=mesh['group'=16,'inner'=8] {'inner'}, dimensions={2} | all-to-all | bytes 442368 | tf_op jit(solution)/shard_map/all_to_all | solution.py:60
  26.8 51.4 %all-gather.4.cloned.1.call-done = bf16[2304,3,256]{2,0,1:T(8,128)(2,1)} async-done(((bf16[144,3,256]{2,0,1:T(8,128)(2,1)}), bf16[2304,3,256]{2,0,1:T(8,128)(2,1)}) %all-gather.4.cloned.1.call-update) | async-done | bytes 3538960 | tf_op jit(solution)/shard_map/all_gather | solution.py:62
  78.2 5.7 %copy.55 = bf16[2304,3,256]{0,2,1:T(8,128)(2,1)} copy(bf16[2304,3,256]{2,0,1:T(8,128)(2,1)} %all-gather.4.cloned.1.call-done) | data formatting | bytes 7077888 | tf_op jit(solution)/shard_map/all_gather | solution.py:62
  84.0 31.8 %all-gather.6.cloned.1.call-done = bf16[512,2304]{1,0:T(8,128)(2,1)} async-done(((bf16[64,2304]{1,0:T(8,128)(2,1)}), bf16[512,2304]{1,0:T(8,128)(2,1)}) %all-gather.6.cloned.1.call-update) | async-done | bytes 2359312 | tf_op jit(solution)/shard_map/all_gather | solution.py:80
  115.8 4.8 fusion.8
  121.6 4.8 fusion.36
  126.5 2.8 fusion.16
  129.3 2.9 fusion.42
  133.6 61.1 %reduce-scatter.5.cloned.1.call-done = f32[64,2304]{1,0:T(8,128)} async-done(((f32[512,2304]{1,0:T(8,128)}), f32[64,2304]{1,0:T(8,128)}) %reduce-scatter.5.cloned.1.call-update) | async-done | bytes 589840 | tf_op jit(solution)/shard_map/reduce_scatter | solution.py:107
  200.9 16.1 %all_to_all.35 = bf16[8,1,20,2304]{3,2,1,0:T(8,128)(2,1)S(1)} all-to-all(bf16[8,1,20,2304]{3,2,1,0:T(8,128)(2,1)S(1)} %bitcast.90), channel_id=1, replica_groups=mesh['group'=16,'inner'=8] {'inner'}, dimensions={0} | all-to-all | bytes 1474560 | tf_op jit(solution)/shard_map/all_to_all | solution.py:132
  218.2 6.9 %convert_element_type.69 = bf16[8,18,2,5760]{3,2,1,0:T(2,128)(2,1)} convert(f32[8,18,2,5760]{3,2,1,0:T(2,128)} %param.16) | non-fusion elementwise | flops 1658880 | bytes 9953280 | tf_op jit(solution)/shard_map/convert_element_type | solution.py:66
  225.1 11.5 %reshape.215 = bf16[8,1,18,2,16,360]{5,4,3,2,0,1:T(8,128)(2,1)} reshape(bf16[8,18,2,5760]{3,2,1,0:T(2,128)(2,1)} %convert_element_type.69) | data formatting | bytes 6635520 | tf_op jit(solution)/shard_map/reshape | solution.py:66
  236.6 4.7 copy.54
  241.4 61.6 %all_to_all.36 = bf16[128,1,1,18,2,360]{5,4,3,2,1,0:T(2,128)(2,1)} all-to-all(bf16[128,1,1,18,2,360]{5,4,3,2,1,0:T(2,128)(2,1)S(1)} %bitcast.87), channel_id=1, replica_groups=mesh['group'=16,'inner'=8] {'group','inner'}, dimensions={0} | all-to-all | bytes 6635520 | tf_op jit(solution)/shard_map/all_to_all | solution.py:71
  302.9 8.5 %reshape_squeeze_reshape.3 = bf16[2304,720]{1,0:T(8,128)(2,1)} reshape(bf16[128,1,1,18,2,360]{5,4,3,2,1,0:T(2,128)(2,1)} %all_to_all.36) | data formatting | bytes 6635520 | tf_op jit(solution)/shard_map/reshape;squeeze;reshape | solution.py:137
  311.4 5.6 %copy.61 = bf16[720,2304]{1,0:T(8,128)(2,1)} copy(bf16[720,2304]{0,1:T(8,128)(2,1)} %bitcast.88) | data formatting | bytes 6635520 | tf_op jit(solution)/shard_map/dot_general | solution.py:136
  317.1 24.8 %all-gather.8.cloned.1.call-done = bf16[128,1,20,2304]{3,0,2,1:T(8,128)(2,1)} async-done(((bf16[8,1,20,2304]{3,0,2,1:T(8,128)(2,1)}), bf16[128,1,20,2304]{3,0,2,1:T(8,128)(2,1)}) %all-gather.8.cloned.1.call-update) | async-done | bytes 11796496 | tf_op jit(solution)/shard_map/all_gather | solution.py:133
  341.9 14.9 %copy.60 = bf16[128,1,20,2304]{3,2,0,1:T(8,128)(2,1)} copy(bf16[128,1,20,2304]{3,0,2,1:T(8,128)(2,1)} %all-gather.8.cloned.1.call-done) | data formatting | bytes 23592960 | tf_op jit(solution)/shard_map/all_gather | solution.py:133
  356.7 17.2 %reshape.226 = bf16[2560,2304,1]{1,0,2:T(8,128)(2,1)} reshape(bf16[128,1,20,2304]{3,2,0,1:T(8,128)(2,1)} %copy.60) | data formatting | bytes 23592960 | tf_op jit(solution)/shard_map/reshape;squeeze | solution.py:135
  373.9 12.7 %fusion.44 = f32[2560,2,360]{0,2,1:T(8,128)S(1)} fusion(bf16[2560,2304,1]{1,0,2:T(8,128)(2,1)} %reshape.226, bf16[2,360,2304]{2,1,0:T(8,128)(2,1)} %bitcast.91), kind=kOutput, calls=%fused_computation.81 | convolution fusion | flops 8493465600 | bytes 22487040 | tf_op jit(solution)/shard_map/dot_general | solution.py:136
  386.6 2.4 fusion.1
  389.0 3.8 copy.62
  392.8 4.0 convert_element_type.82
  396.8 8.3 %fusion.37 = bf16[16,8,20,2304]{3,1,0,2:T(8,128)(2,1)S(1)} fusion(bf16[1,360,2304]{2,1,0:T(8,128)(2,1)S(1)} %copy-done, bf16[128,20,360]{2,1,0:T(8,128)(2,1)} %convert_element_type.82), kind=kOutput, calls=%fused_computation.78 | convolution fusion | flops 4252631040 | bytes 15298560 | tf_op jit(solution)/shard_map/dot_general | solution.py:141
  405.1 5.0 copy.72
  410.5 113.2 %reduce-scatter.7.cloned.1.call-done = bf16[8,46080]{1,0:T(8,128)(2,1)} async-done(((bf16[128,46080]{1,0:T(8,128)(2,1)}), bf16[8,46080]{1,0:T(8,128)(2,1)}) %reduce-scatter.7.cloned.1.call-update) | async-done | bytes 737296
  523.6 2.2 copy.64
  525.8 4.2 all-to-all-start.3
  530.1 10.4 %copy.65 = bf16[1,2304,2,360]{1,3,2,0:T(8,128)(2,1)} copy(bf16[1,2304,2,360]{3,2,1,0:T(2,128)(2,1)} %bitcast.86) | data formatting | bytes 6635520
  540.7 3.4 all-to-all-done.3
  547.5 1.8 copy.81
  (72 shorter events, 17.9 us)
Async XLA Ops:
  7.2 389.6 %copy-start = (bf16[1,360,2304]{2,1,0:T(8,128)(2,1)S(1)}, bf16[1,360,2304]{2,1,0:T(8,128)(2,1)}, u32[]{:S(2)}) copy-start(bf16[1,360,2304]{2,1,0:T(8,128)(2,1)} %param.18) | copy-start | bytes 4976644
  7.2 15.3 %copy-start.2 = (bf16[1,64,2304]{2,1,0:T(8,128)(2,1)S(1)}, bf16[1,64,2304]{2,1,0:T(8,128)(2,1)}, u32[]{:S(2)}) copy-start(bf16[1,64,2304]{2,1,0:T(8,128)(2,1)} %param.11) | copy-start | bytes 884740
  7.2 15.5 %copy-start.11 = (f32[2304]{0:T(1024)S(1)}, f32[2304]{0:T(1024)}, u32[]{:S(2)}) copy-start(f32[2304]{0:T(1024)} %param.19) | copy-start | bytes 27652
  7.2 71.0 %all-gather.4.cloned.1.call-start = ((), (), s32[]{:S(2)}) async-start(), calls=%async_computation.6 | async-start | bytes 3760128 | tf_op jit(solution)/shard_map/all_gather | solution.py:62
  22.4 93.4 %all-gather.6.cloned.1.call-start = ((), (), s32[]{:S(2)}) async-start(), calls=%async_computation.7 | async-start | bytes 2654208 | tf_op jit(solution)/shard_map/all_gather | solution.py:80
  23.5 171.1 %reduce-scatter.5.cloned.1.call-start = ((), (), s32[]{:S(2)}) async-start(), calls=%async_computation.8 | async-start | bytes 5308416 | tf_op jit(solution)/shard_map/reduce_scatter | solution.py:107
  115.8 4.9 copy-start.7
  115.8 4.9 copy-start.8
  126.5 2.8 copy-start.6
  132.2 0.7 copy-start.12
  132.2 63.7 %copy-start.10 = (f32[2304]{0:T(1024)S(1)}, f32[2304]{0:T(1024)}, u32[]{:S(2)}) copy-start(f32[2304]{0:T(1024)} %param.20) | copy-start | bytes 27652
  132.3 209.6 %all-gather.8.cloned.1.call-start = ((), (), s32[]{:S(2)}) async-start(), calls=%async_computation.9 | async-start | bytes 12533760 | tf_op jit(solution)/shard_map/all_gather | solution.py:133
  197.1 0.7 copy-start.4
  218.0 305.7 %reduce-scatter.7.cloned.1.call-start = ((), (), s32[]{:S(2)}) async-start(), calls=%async_computation.10 | async-start | bytes 12533760
  525.8 18.3 %all-to-all-start.3 = ((bf16[8,1,20,2304]{3,2,1,0:T(8,128)(2,1)}), bf16[8,1,20,2304]{3,2,1,0:T(8,128)(2,1)}, u32[]{:S(2)}, u32[]{:S(2)}) async-start(bf16[8,1,20,2304]{3,2,1,0:T(8,128)(2,1)} %copy.64), calls=%async_computation.4 | async-start | bytes 1769472 | tf_op jit(solution)/shard_map/all_to_all | solution.py:145
  530.0 10.5 %copy-start.5 = (bf16[64,2304]{1,0:T(8,128)(2,1)S(1)}, bf16[64,2304]{1,0:T(8,128)(2,1)}, u32[]{:S(2)}) copy-start(bf16[64,2304]{1,0:T(8,128)(2,1)} %copy-done.4) | copy-start | bytes 884740
  530.0 10.5 %copy-start.9 = (bf16[2304,8]{0,1:T(8,128)(2,1)S(1)}, bf16[2304,8]{0,1:T(8,128)(2,1)}, u32[]{:S(2)}) copy-start(bf16[2304,8]{0,1:T(8,128)(2,1)} %param.21) | copy-start | bytes 110596
  530.1 15.6 %copy-start.3 = (f32[64,2304]{1,0:T(8,128)S(1)}, f32[64,2304]{1,0:T(8,128)}, u32[]{:S(2)}) copy-start(f32[64,2304]{1,0:T(8,128)} %reduce-scatter.5.cloned.1.call-done) | copy-start | bytes 1769476
  545.4 2.1 copy-start.1
Sparse Core Ops, SparseCore 0:
  22.5 55.6 all-gather.3
  80.4 35.3 all-gather.5
  132.4 62.2 reduce-scatter.4
  218.1 123.7 all-gather.7
  410.3 113.3 reduce-scatter.6
where the time goes:
time: 558 us; the launch traced here: 556 us
  waiting for transfers between devices  286 us (51%)
  local copies, waits for them, and re-layouts  103 us (18%)
  blocking collectives  90.4 us (16%)
  matrix products  39.1 us (7%)
  other arithmetic  17.4 us (3%)
  between operations  15.4 us (3%)
    unnamed x6, waiting for transfers between devices  113 us
    all_to_all x1, blocking collectives, body(): lax.all_to_all(joined, ('group', 'inner'), split_axis=0, concat_axis=2, t...  61.6 us
    reduce_scatter x1, waiting for transfers between devices, body(): lax.psum_scatter(jnp.dot(block_outputs, out_weight, preferred_element_typ...  61.1 us
    all_gather x1, waiting for transfers between devices, body(): server_qkv = lax.all_gather(head_parts, 'group', axis=0, tiled=True)  51.4 us
    all_gather x1, waiting for transfers between devices, body(): piece_rows = lax.all_gather(normed, 'inner', axis=0, tiled=True)  31.8 us
    all_gather x1, waiting for transfers between devices, body(): arrived = lax.all_gather(owned, 'group', axis=0, tiled=True)  24.8 us
    unnamed x30, local copies, waits for them, and re-layouts  19.4 us
    another operation x1, local copies, waits for them, and re-layouts, body(): rows_in = arrived[:, 0].reshape(item_count * capacity, D)  17.2 us
  transfers between devices with their start and end apart: 6, of which 6 were waited for; matrix products, arithmetic and copies ran while one was open for 10% of the time, Pallas kernels for 0%

commit v1 on v0

--- a/solution.py
+++ b/solution.py
@@ -59,7 +59,9 @@
     cast_qkv = trainer_qkv.astype(jnp.bfloat16).reshape(row_share, 3, inner_size, head_block)
     head_parts = lax.all_to_all(cast_qkv, "inner", split_axis=2, concat_axis=0, tiled=True)
     head_parts = head_parts.reshape(inner_size * row_share, 3, head_block)
-    server_qkv = lax.all_gather(head_parts, "group", axis=0, tiled=True)
+    server_qkv = jnp.concatenate(
+        lax.all_to_all(jnp.stack([head_parts] * lax.axis_size("group")), "group", 0, 0), axis=0
+    )
     expert_count = trainer_gate_up.shape[0]
     local_experts = expert_count // inner_size
     hidden_share = trainer_gate_up.shape[3] // group_size

time: 558 us -> 539 us (0.966)
  waiting for transfers between devices: 286 us -> 246 us
  local copies, waits for them, and re-layouts: 103 us -> 114 us
  starting transfers between devices: 4.61 us -> 14.1 us
    all_gather x1 -> x0, waiting for transfers between devices: 51.4 us -> none  [body(): server_qkv = lax.all_gather(head_parts, 'group', axis=0, tiled=True)]
    all_to_all x0 -> x1, waiting for transfers between devices: none -> 51.4 us  [body(): lax.all_to_all(jnp.stack([head_parts] * lax.axis_size('group')), 'group',...]
    all_gather x1, waiting for transfers between devices: 31.8 us -> 0.01 us  [body(): piece_rows = lax.all_gather(normed, 'inner', axis=0, tiled=True)]
    all_to_all x0 -> x1, starting transfers between devices: none -> 9.71 us  [body(): lax.all_to_all(jnp.stack([head_parts] * lax.axis_size('group')), 'group',...]
    all_to_all x0 -> x2, local copies, waits for them, and re-layouts: none -> 8.64 us  [body(): lax.all_to_all(jnp.stack([head_parts] * lax.axis_size('group')), 'group',...]
    dot_general x0 -> x1, local copies, waits for them, and re-layouts: none -> 5.79 us  [body(): jnp.dot(piece_rows, flat_qkv, preferred_element_type=jnp.float32)]
    all_gather x1 -> x0, local copies, waits for them, and re-layouts: 5.74 us -> none  [body(): server_qkv = lax.all_gather(head_parts, 'group', axis=0, tiled=True)]
    unnamed x30 -> x26, local copies, waits for them, and re-layouts: 19.4 us -> 19.7 us
  transfers between devices with their start and end apart: 6 -> 6, of which waited for: 6 -> 4; matrix products, arithmetic and copies ran while one was open for 10% -> 13% of each run, Pallas kernels for 0% -> 0%
where the time goes in v1:
time: 539 us; the launch traced here: 537 us
  waiting for transfers between devices  246 us (46%)
  local copies, waits for them, and re-layouts  114 us (21%)
  blocking collectives  90.6 us (17%)
  matrix products  38.9 us (7%)
  other arithmetic  18.6 us (3%)
  between operations  15.3 us (3%)
  starting transfers between devices  14.1 us (3%)
    unnamed x5, waiting for transfers between devices  113 us
    all_to_all x1, blocking collectives, body(): lax.all_to_all(joined, ('group', 'inner'), split_axis=0, concat_axis=2, t...  61.4 us
    reduce_scatter x1, waiting for transfers between devices, body(): lax.psum_scatter(jnp.dot(block_outputs, out_weight, preferred_element_typ...  56.3 us
    all_to_all x1, waiting for transfers between devices, body(): lax.all_to_all(jnp.stack([head_parts] * lax.axis_size('group')), 'group',...  51.4 us
    all_gather x1, waiting for transfers between devices, body(): arrived = lax.all_gather(owned, 'group', axis=0, tiled=True)  24.8 us
    unnamed x26, local copies, waits for them, and re-layouts  19.7 us
    another operation x1, local copies, waits for them, and re-layouts, body(): rows_in = arrived[:, 0].reshape(item_count * capacity, D)  17.2 us
    all_to_all x1, blocking collectives, body(): lax.all_to_all(send_rows, 'inner', split_axis=0, concat_axis=0, tiled=True)  16.4 us
  transfers between devices with their start and end apart: 6, of which 4 were waited for; matrix products, arithmetic and copies ran while one was open for 13% of the time, Pallas kernels for 0%

profile of v1, /device:TPU:1, one launch (start us, length us, event | category | flops | bytes accessed | tf_op | source)
XLA Modules:
  0.0 536.6 jit_solution(7101737163148010467)
XLA Ops:
  11.8 12.7 %all_to_all.39 = bf16[18,3,8,256]{3,0,1,2:T(8,128)(2,1)S(1)} all-to-all(bf16[18,3,8,256]{3,0,1,2:T(8,128)(2,1)S(1)} %copy.74), channel_id=1, replica_groups=mesh['group'=16,'inner'=8] {'inner'}, dimensions={2} | all-to-all | bytes 442368 | tf_op jit(solution)/shard_map/all_to_all | solution.py:60
  26.7 9.7 %all-to-all-start.1 = ((bf16[16,144,3,256]{3,1,2,0:T(8,128)(2,1)}), bf16[16,144,3,256]{3,1,2,0:T(8,128)(2,1)}, u32[]{:S(2)}, u32[]{:S(2)}) async-start(bf16[16,144,3,256]{3,1,2,0:T(8,128)(2,1)} %stack.3), calls=%async_computation.1 | async-start | bytes 7077888 | tf_op jit(solution)/shard_map/all_to_all | solution.py:63
  38.9 51.4 %all-to-all-done.1 = bf16[16,144,3,256]{3,1,2,0:T(8,128)(2,1)} async-done(((bf16[16,144,3,256]{3,1,2,0:T(8,128)(2,1)}), bf16[16,144,3,256]{3,1,2,0:T(8,128)(2,1)}, u32[]{:S(2)}, u32[]{:S(2)}) %all-to-all-start.1) | async-done | bytes 3538976 | tf_op jit(solution)/shard_map/all_to_all | solution.py:63
  90.3 4.4 copy.78
  94.7 2.8 copy.96
  97.6 5.8 %copy.79 = bf16[768,2304]{1,0:T(8,128)(2,1)} copy(bf16[768,2304]{0,1:T(8,128)(2,1)} %bitcast.91) | data formatting | bytes 7077888 | tf_op jit(solution)/shard_map/dot_general | solution.py:84
  103.4 4.8 fusion.8
  109.2 4.7 fusion.36
  113.9 2.8 fusion.16
  116.8 2.9 fusion.42
  121.1 56.3 %reduce-scatter.5.cloned.1.call-done = f32[64,2304]{1,0:T(8,128)} async-done(((f32[512,2304]{1,0:T(8,128)}), f32[64,2304]{1,0:T(8,128)}) %reduce-scatter.5.cloned.1.call-update) | async-done | bytes 589840 | tf_op jit(solution)/shard_map/reduce_scatter | solution.py:109
  183.6 16.4 %all_to_all.40 = bf16[8,1,20,2304]{3,2,1,0:T(8,128)(2,1)S(1)} all-to-all(bf16[8,1,20,2304]{3,2,1,0:T(8,128)(2,1)S(1)} %bitcast.95), channel_id=1, replica_groups=mesh['group'=16,'inner'=8] {'inner'}, dimensions={0} | all-to-all | bytes 1474560 | tf_op jit(solution)/shard_map/all_to_all | solution.py:134
  201.1 6.9 %convert_element_type.69 = bf16[8,18,2,5760]{3,2,1,0:T(2,128)(2,1)} convert(f32[8,18,2,5760]{3,2,1,0:T(2,128)} %param.16) | non-fusion elementwise | flops 1658880 | bytes 9953280 | tf_op jit(solution)/shard_map/convert_element_type | solution.py:68
  207.9 11.5 %reshape.214 = bf16[8,1,18,2,16,360]{5,4,3,2,0,1:T(8,128)(2,1)} reshape(bf16[8,18,2,5760]{3,2,1,0:T(2,128)(2,1)} %convert_element_type.69) | data formatting | bytes 6635520 | tf_op jit(solution)/shard_map/reshape | solution.py:68
  219.5 4.7 copy.77
  224.2 61.4 %all_to_all.41 = bf16[128,1,1,18,2,360]{5,4,3,2,1,0:T(2,128)(2,1)} all-to-all(bf16[128,1,1,18,2,360]{5,4,3,2,1,0:T(2,128)(2,1)S(1)} %bitcast.90), channel_id=1, replica_groups=mesh['group'=16,'inner'=8] {'group','inner'}, dimensions={0} | all-to-all | bytes 6635520 | tf_op jit(solution)/shard_map/all_to_all | solution.py:73
  285.6 8.5 %reshape_squeeze_reshape.3 = bf16[2304,720]{1,0:T(8,128)(2,1)} reshape(bf16[128,1,1,18,2,360]{5,4,3,2,1,0:T(2,128)(2,1)} %all_to_all.41) | data formatting | bytes 6635520 | tf_op jit(solution)/shard_map/reshape;squeeze;reshape | solution.py:139
  294.1 5.7 %copy.85 = bf16[720,2304]{1,0:T(8,128)(2,1)} copy(bf16[720,2304]{0,1:T(8,128)(2,1)} %bitcast.92) | data formatting | bytes 6635520 | tf_op jit(solution)/shard_map/dot_general | solution.py:138
  299.8 24.8 %all-gather.5.cloned.1.call-done = bf16[128,1,20,2304]{3,0,2,1:T(8,128)(2,1)} async-done(((bf16[8,1,20,2304]{3,0,2,1:T(8,128)(2,1)}), bf16[128,1,20,2304]{3,0,2,1:T(8,128)(2,1)}) %all-gather.5.cloned.1.call-update) | async-done | bytes 11796496 | tf_op jit(solution)/shard_map/all_gather | solution.py:135
  324.5 14.8 %copy.84 = bf16[128,1,20,2304]{3,2,0,1:T(8,128)(2,1)} copy(bf16[128,1,20,2304]{3,0,2,1:T(8,128)(2,1)} %all-gather.5.cloned.1.call-done) | data formatting | bytes 23592960 | tf_op jit(solution)/shard_map/all_gather | solution.py:135
  339.3 17.2 %reshape.224 = bf16[2560,2304,1]{1,0,2:T(8,128)(2,1)} reshape(bf16[128,1,20,2304]{3,2,0,1:T(8,128)(2,1)} %copy.84) | data formatting | bytes 23592960 | tf_op jit(solution)/shard_map/reshape;squeeze | solution.py:137
  356.5 12.7 %fusion.44 = f32[2560,2,360]{0,2,1:T(8,128)S(1)} fusion(bf16[2560,2304,1]{1,0,2:T(8,128)(2,1)} %reshape.224, bf16[2,360,2304]{2,1,0:T(8,128)(2,1)} %bitcast.96), kind=kOutput, calls=%fused_computation.81 | convolution fusion | flops 8493465600 | bytes 22487040 | tf_op jit(solution)/shard_map/dot_general | solution.py:138
  369.2 2.4 fusion.1
  371.6 3.8 copy.86
  375.4 4.0 convert_element_type.82
  379.4 8.3 %fusion.37 = bf16[16,8,20,2304]{3,1,0,2:T(8,128)(2,1)S(1)} fusion(bf16[1,360,2304]{2,1,0:T(8,128)(2,1)S(1)} %copy-done, bf16[128,20,360]{2,1,0:T(8,128)(2,1)} %convert_element_type.82), kind=kOutput, calls=%fused_computation.78 | convolution fusion | flops 4252631040 | bytes 15298560 | tf_op jit(solution)/shard_map/dot_general | solution.py:143
  387.7 5.1 copy.97
  393.2 113.0 %reduce-scatter.7.cloned.1.call-done = bf16[8,46080]{1,0:T(8,128)(2,1)} async-done(((bf16[128,46080]{1,0:T(8,128)(2,1)}), bf16[8,46080]{1,0:T(8,128)(2,1)}) %reduce-scatter.7.cloned.1.call-update) | async-done | bytes 737296
  506.2 2.2 copy.88
  508.4 4.2 all-to-all-start.4
  512.6 10.3 %copy.89 = bf16[1,2304,2,360]{1,3,2,0:T(8,128)(2,1)} copy(bf16[1,2304,2,360]{3,2,1,0:T(2,128)(2,1)} %bitcast.88) | data formatting | bytes 6635520
  523.0 4.2 copy.76
  (70 shorter events, 20.7 us)
Async XLA Ops:
  7.2 372.2 %copy-start = (bf16[1,360,2304]{2,1,0:T(8,128)(2,1)S(1)}, bf16[1,360,2304]{2,1,0:T(8,128)(2,1)}, u32[]{:S(2)}) copy-start(bf16[1,360,2304]{2,1,0:T(8,128)(2,1)} %param.18) | copy-start | bytes 4976644
  7.2 96.2 %all-gather.3.cloned.1.call-start = ((), (), s32[]{:S(2)}) async-start(), calls=%async_computation.7 | async-start | bytes 2654208 | tf_op jit(solution)/shard_map/all_gather | solution.py:82
  26.7 63.6 %all-to-all-start.1 = ((bf16[16,144,3,256]{3,1,2,0:T(8,128)(2,1)}), bf16[16,144,3,256]{3,1,2,0:T(8,128)(2,1)}, u32[]{:S(2)}, u32[]{:S(2)}) async-start(bf16[16,144,3,256]{3,1,2,0:T(8,128)(2,1)} %stack.3), calls=%async_computation.1 | async-start | bytes 7077888 | tf_op jit(solution)/shard_map/all_to_all | solution.py:63
  36.4 141.0 %reduce-scatter.5.cloned.1.call-start = ((), (), s32[]{:S(2)}) async-start(), calls=%async_computation.8 | async-start | bytes 5308416 | tf_op jit(solution)/shard_map/reduce_scatter | solution.py:109
  103.4 4.9 copy-start.6
  103.4 4.9 copy-start.7
  113.9 2.8 copy-start.5
  119.7 0.7 copy-start.10
  119.7 57.7 %copy-start.1 = (bf16[1,64,2304]{2,1,0:T(8,128)(2,1)S(1)}, bf16[1,64,2304]{2,1,0:T(8,128)(2,1)}, u32[]{:S(2)}) copy-start(bf16[1,64,2304]{2,1,0:T(8,128)(2,1)} %param.11) | copy-start | bytes 884740
  119.7 59.0 %copy-start.9 = (f32[2304]{0:T(1024)S(1)}, f32[2304]{0:T(1024)}, u32[]{:S(2)}) copy-start(f32[2304]{0:T(1024)} %param.20) | copy-start | bytes 27652
  119.7 204.8 %all-gather.5.cloned.1.call-start = ((), (), s32[]{:S(2)}) async-start(), calls=%async_computation.9 | async-start | bytes 12533760 | tf_op jit(solution)/shard_map/all_gather | solution.py:135
  179.9 0.7 copy-start.3
  201.0 305.2 %reduce-scatter.7.cloned.1.call-start = ((), (), s32[]{:S(2)}) async-start(), calls=%async_computation.10 | async-start | bytes 12533760
  508.4 19.1 %all-to-all-start.4 = ((bf16[8,1,20,2304]{3,2,1,0:T(8,128)(2,1)}), bf16[8,1,20,2304]{3,2,1,0:T(8,128)(2,1)}, u32[]{:S(2)}, u32[]{:S(2)}) async-start(bf16[8,1,20,2304]{3,2,1,0:T(8,128)(2,1)} %copy.88), calls=%async_computation.5 | async-start | bytes 1769472 | tf_op jit(solution)/shard_map/all_to_all | solution.py:147
  523.0 4.2 copy-start.4
  523.0 4.2 copy-start.8
  523.0 6.1 %copy-start.2 = (f32[64,2304]{1,0:T(8,128)S(1)}, f32[64,2304]{1,0:T(8,128)}, u32[]{:S(2)}) copy-start(f32[64,2304]{1,0:T(8,128)} %reduce-scatter.5.cloned.1.call-done) | copy-start | bytes 1769476
Sparse Core Ops, SparseCore 0:
  10.4 44.2 all-gather.2
  119.8 57.5 reduce-scatter.4
  201.1 123.3 all-gather.4
  393.0 113.1 reduce-scatter.6
